TPU v7x, 32 devices: a whole 2x2x4 slice. The times are simulated.
32 devices in a mesh: gx: 4 (over y, x), gy: 8 (over z, core).
Axes of the slice: x: 2, y: 2, z: 4, core: 2. Of those that a mesh axis runs over, the one named last changes fastest.
Arguments:
- old_state: float32 [8, 8, 128, 1024], P(None, None, 'gx', 'gy'), may hold values from -6 to 6
- section_prims: float32 [8, 8, 128, 1024], P(None, None, 'gx', 'gy'), may hold values from -3 to 3, as said below
- shear_whole: int32 [1], replicated, may hold values from 0 to 1023
- shear_frac: float32 [1], replicated, may hold values from 0 to 1
Outputs:
- new_state: float32 [8, 8, 128, 1024], P(None, None, 'gx', 'gy')
Inputs may be any that keep to these rules, and one draw needn't show every extreme that they name: section_prims holds density in [0.5, 2] in field 0 and pressure in [0.3, 3] in field 4; the other fields lie in the stated range.
All inputs are finite; a program needn't handle non-finite values.
Results may differ from a plain program's by a relative error of at most 0.0003.
Values sent between devices are 32-bit elements; how exact they have to be, the bound alone decides.
No kernel may reach another device: no remote copies, remote signals or barrier semaphores. Data moves between devices by JAX's collectives and lax.ppermute only.
A program may use at most 128 MiB of HBM per device.

v0:
```python
import jax
import jax.numpy as jnp
from jax import lax
from jax.sharding import PartitionSpec as P

gamma_gas = 5.0 / 3.0
omega_rate = 1.0
shear_rate = 1.5
time_step = 0.1


def with_halo(shard, sides, width):
    for axis, dim in sides:
        size, length = (lax.axis_size(axis), shard.shape[dim])
        up = [(i, (i + 1) % size) for i in range(size)]
        down = [(j, i) for i, j in up]
        last = lax.slice_in_dim(shard, length - width, length, axis=dim)
        first = lax.slice_in_dim(shard, 0, width, axis=dim)
        before = lax.ppermute(last, axis, up)
        after = lax.ppermute(first, axis, down)
        shard = jnp.concatenate([before, shard, after], axis=dim)
    return shard


def conserved(prims):
    rho = prims[0]
    kinetic = 0.5 * rho * (prims[1] * prims[1] + prims[2] * prims[2] + prims[3] * prims[3])
    magnetic = 0.5 * (prims[5] * prims[5] + prims[6] * prims[6] + prims[7] * prims[7])
    energy = prims[4] / (gamma_gas - 1.0) + kinetic + magnetic
    return jnp.stack(
        [rho, rho * prims[1], rho * prims[2], rho * prims[3], energy, prims[5], prims[6], prims[7]]
    )


def fluxes(prims, cons, direction):
    rho = prims[0]
    normal_vel = prims[1 + direction]
    normal_mag = prims[5 + direction]
    ptotal = prims[4] + 0.5 * (prims[5] * prims[5] + prims[6] * prims[6] + prims[7] * prims[7])
    vdotb = prims[1] * prims[5] + prims[2] * prims[6] + prims[3] * prims[7]
    parts = [rho * normal_vel]
    for comp in range(3):
        parts.append(rho * prims[1 + comp] * normal_vel - prims[5 + comp] * normal_mag)
    parts[1 + direction] = parts[1 + direction] + ptotal
    parts.append((cons[4] + ptotal) * normal_vel - normal_mag * vdotb)
    for comp in range(3):
        parts.append(prims[5 + comp] * normal_vel - prims[1 + comp] * normal_mag)
    return jnp.stack(parts)


def fast_speed(prims, direction):
    rho = prims[0]
    sound = gamma_gas * prims[4] / rho
    squares = [prims[5] * prims[5], prims[6] * prims[6], prims[7] * prims[7]]
    alfven = (squares[0] + squares[1] + squares[2]) / rho
    others = [squares[c] for c in range(3) if c != direction]
    transverse = (others[0] + others[1]) / rho
    disc = jnp.square(sound - alfven) + 4.0 * sound * transverse
    return jnp.sqrt(0.5 * (sound + alfven + jnp.sqrt(disc)))


def minmod(first, second):
    return 0.5 * (jnp.sign(first) + jnp.sign(second)) * jnp.minimum(jnp.abs(first), jnp.abs(second))


def rusanov(left, right, direction):
    cons_left = conserved(left)
    cons_right = conserved(right)
    flux_left = fluxes(left, cons_left, direction)
    flux_right = fluxes(right, cons_right, direction)
    speed_left = jnp.abs(left[1 + direction]) + fast_speed(left, direction)
    speed_right = jnp.abs(right[1 + direction]) + fast_speed(right, direction)
    speed = jnp.maximum(speed_left, speed_right)
    return 0.5 * (flux_left + flux_right) - 0.5 * speed * (cons_right - cons_left)


def sweep(padded, axis, direction):
    length = padded.shape[axis]
    cells = length - 4

    def take(arr, start, stop):
        return lax.slice_in_dim(arr, start, stop, axis=axis)

    diff = take(padded, 1, length) - take(padded, 0, length - 1)
    slope = minmod(take(diff, 0, length - 2), take(diff, 1, length - 1))
    left = take(padded, 1, length - 2) + 0.5 * take(slope, 0, length - 3)
    right = take(padded, 2, length - 1) - 0.5 * take(slope, 1, length - 2)
    face = rusanov(left, right, direction)
    return take(face, 1, cells + 1) - take(face, 0, cells)


def sources(core):
    rho = core[0]
    zeros = jnp.zeros_like(rho)
    return jnp.stack(
        [
            zeros,
            2.0 * omega_rate * rho * core[2],
            -(2.0 - shear_rate) * omega_rate * rho * core[1],
            zeros,
            shear_rate * omega_rate * (rho * core[1] * core[2] - core[5] * core[6]),
            zeros,
            -shear_rate * omega_rate * core[5],
            zeros,
        ]
    )


def section_update(radial_rows, azimuthal_rows, old):
    core = azimuthal_rows[:, :, :, 2:-2]
    radial = sweep(radial_rows, 2, 0)
    azimuthal = sweep(azimuthal_rows, 3, 1)
    zpadded = jnp.concatenate([core[:, -2:], core, core[:, :2]], axis=1)
    vertical = sweep(zpadded, 1, 2)
    rates = -(radial + azimuthal + vertical) + sources(core)
    return 0.5 * old + 0.5 * (conserved(core) + time_step * rates)


def on_device(old_state, section_prims, shear_whole, shear_frac):
    padded = with_halo(section_prims, (("gx", 2), ("gy", 3)), 2)
    cells = section_prims.shape[3]
    loop_size = lax.axis_size("gy")
    total = cells * loop_size
    shift_cells = shear_whole[0]
    frac = shear_frac[0]
    back_cells = (total - 1 - shift_cells) % total
    inner_src = padded[:, :, 0:2, 2:-2]
    outer_src = padded[:, :, -2:, 2:-2]
    inner_cycle, outer_cycle = (
        lax.all_gather(inner_src, "gy", axis=3, tiled=True),
        lax.all_gather(outer_src, "gy", axis=3, tiled=True),
    )
    position = lax.axis_index("gy") * cells
    inner_ext = jnp.concatenate([inner_cycle, inner_cycle[..., : cells + 1]], axis=3)
    outer_ext = jnp.concatenate([outer_cycle, outer_cycle[..., : cells + 1]], axis=3)
    inner_win = lax.dynamic_slice_in_dim(inner_ext, (position + shift_cells) % total, cells + 1, 3)
    outer_win = lax.dynamic_slice_in_dim(outer_ext, (position + back_cells) % total, cells + 1, 3)
    inner_ghost = (1.0 - frac) * inner_win[..., :cells] + frac * inner_win[..., 1:]
    outer_ghost = (1.0 - frac) * outer_win[..., 1:] + frac * outer_win[..., :cells]
    radial_index = lax.axis_index("gx")
    left_rows = jnp.where(radial_index == 0, inner_ghost, inner_src)
    right_rows = jnp.where(radial_index == lax.axis_size("gx") - 1, outer_ghost, outer_src)
    azimuthal_rows = padded[:, :, 2:-2, :]
    radial_rows = jnp.concatenate([left_rows, azimuthal_rows[:, :, :, 2:-2], right_rows], axis=2)
    return section_update(radial_rows, azimuthal_rows, old_state)


def solution(mesh):
    in_specs = (P(None, None, "gx", "gy"), P(None, None, "gx", "gy"), P(), P())
    out_specs = P(None, None, "gx", "gy")
    return jax.shard_map(
        on_device, mesh=mesh, in_specs=in_specs, out_specs=out_specs, check_vma=False
    )
```

profile of v0, /device:TPU:0, one launch (start us, length us, event | category | flops | bytes accessed | tf_op | source)
XLA Modules:
  0.0 111.1 jit_solution(10720879476394507808)
XLA Ops:
  0.0 1.9 %copy.188 = f32[8,8,32,128]{3,1,2,0:T(8,128)S(1)} copy(f32[8,8,32,128]{3,2,1,0:T(8,128)} %param.5) | data formatting | bytes 2097152 | tf_op args[1]
  1.9 1.0 copy-done.4
  3.6 3.9 %collective-permute-start.1 = (f32[8,8,2,128]{3,1,2,0:T(8,128)}, f32[8,8,2,128]{3,1,2,0:T(8,128)S(1)}, u32[]{:S(2)}, u32[]{:S(2)}) collective-permute-start(f32[8,8,2,128]{3,1,2,0:T(8,128)} %get-tuple-element.78), channel_id=1, source_target_pairs={{8,0},{16,8},{24,16},{0,24},{9,1},{17,9},{25,17},{1,25},{10,2},{18... | collective-permute-start | bytes 196616 | tf_op jit(solution)/shard_map/ppermute | solution.py:20
  8.4 1.7 %pad_maximum_fusion.5 = (f32[8,9,32,128]{3,2,1,0:T(8,128)}, f32[8,9,32,128]{3,2,1,0:T(8,128)}) fusion(f32[8,8,32,128]{3,2,1,0:T(8,128)S(1)} %copy-done.1, f32[8,2,32,128]{3,2,1,0:T(8,128)S(1)} %get-tuple-element.82, f32[8,2,32,128]{3,2,1,0:T(8,128)S(1)} %get-tuple-element.83), kind=kLoop, calls=%fused_computation.19 | loop fusion | flops 589824 | bytes 3932160 | tf_op jit(solution)/shard_map/concatenate | solution.py:113
  12.4 2.1 %copy_subtract_fusion = f32[8,11,32,128]{3,1,2,0:T(8,128)S(1)} fusion(f32[8,11,32,128]{3,2,1,0:T(8,128)S(1)} %get-tuple-element.51, f32[8,11,32,128]{3,2,1,0:T(8,128)S(1)} %get-tuple-element.50), kind=kLoop, calls=%fused_computation.12 | loop fusion | flops 360448 | bytes 4325376 | tf_op jit(solution)/shard_map/sub | solution.py:84
  14.5 1.5 %minimum_multiply_fusion = f32[8,10,32,128]{3,1,2,0:T(8,128)S(1)} fusion(f32[8,11,32,128]{3,1,2,0:T(8,128)S(1)} %copy_subtract_fusion), kind=kLoop, calls=%fused_computation.14 | loop fusion | flops 2621440 | bytes 3932160 | tf_op jit(solution)/shard_map/mul | solution.py:63
  16.1 2.2 %fusion.1 = (f32[8,9,32,128]{3,1,2,0:T(8,128)S(1)}, f32[8,9,32,128]{3,1,2,0:T(8,128)S(1)}) fusion(f32[8,10,32,128]{3,1,2,0:T(8,128)S(1)} %minimum_multiply_fusion, f32[8,9,32,128]{3,2,1,0:T(8,128)S(1)} %copy-done.8, f32[8,9,32,128]{3,2,1,0:T(8,128)S(1)} %copy-done.9), kind=kLoop, calls=%fused_computation.4 | loop fusion | flops 1179648 | bytes 7077888 | tf_op jit(solution)/shard_map/add | solution.py:86
  18.5 1.3 %multiply_bitcast_fusion = (f32[9,32,128]{2,0,1:T(8,128)}, f32[1,9,32,128]{3,1,2,0:T(8,128)S(1)}, f32[1,9,32,128]{3,1,2,0:T(8,128)S(1)}, f32[8,9,32,128]{3,1,2,0:T(8,128)S(1)}) fusion(f32[8,9,32,128]{3,1,2,0:T(8,128)S(1)} %get-tuple-element.49, f32[8,9,32,128]{3,1,2,0:T(8,128)S(1)} %get-tuple-element.48, ...), kind=kLoop, calls=%fused_computation.52 | loop fusion | flops 1622016 | bytes 4341760 | tf_op jit(solution)/shard_map/mul | solution.py:74
  23.6 0.9 subtract_dynamic-update-slice_fusion.9
  31.2 0.8 constant_dynamic-update-slice_fusion.59
  32.0 0.8 slice_dynamic-update-slice_fusion.6
  33.6 2.1 %constant_dynamic-update-slice_fusion.53 = f32[8,9,32,128]{3,1,2,0:T(8,128)} fusion(f32[8,9,32,128]{3,1,2,0:T(8,128)} %constant_dynamic-update-slice_fusion.54, f32[1,9,32,128]{3,1,2,0:T(8,128)} %get-tuple-element.25), kind=kLoop, calls=%fused_computation.157 | loop fusion | bytes 524288
  35.7 2.5 %slice_dynamic-update-slice_fusion = (f32[8,9,32,128]{3,1,2,0:T(8,128)}, f32[8,9,32,128]{3,1,2,0:T(8,128)}) fusion(f32[8,9,32,128]{3,1,2,0:T(8,128)} %constant_dynamic-update-slice_fusion.53, f32[8,9,32,128]{3,1,2,0:T(8,128)} %copy-done, f32[8,9,32,128]{3,1,2,0:T(8,128)} %constant_dynamic-update-slice_fusion.48, f32[8,9,32,128]{3,1,2,0:T(8,128)S(1)} %get-tuple-element.49), kind=kLoop, calls=%fused_computation.41 | loop fusion | bytes 2801664 | tf_op jit(solution)/shard_map/stack | solution.py:30
  38.2 4.1 %multiply_subtract_fusion = f32[8,9,32,128]{3,1,2,0:T(8,128)} fusion(f32[8,9,32,128]{3,1,2,0:T(8,128)} %get-tuple-element.89, f32[8,9,32,128]{3,1,2,0:T(8,128)} %get-tuple-element.88, f32[8,9,32,128]{3,1,2,0:T(8,128)S(1)} %copy-done.13, f32[8,9,32,128]{3,1,2,0:T(8,128)S(1)} %copy-done.11, f32[9,32,128]{2,0,1:T(8,128)} %get-tuple-element.19), kind=kLoop, calls=%fused_computation.13 | loop fusion | flops 1474560 | bytes 6045696 | tf_op jit(solution)/shard_map/sub | solution.py:74
  43.0 15.0 %all_gather.7 = f32[8,8,2,1024]{3,1,2,0:T(8,128)S(1)} all-gather(f32[8,8,2,128]{3,1,2,0:T(8,128)S(1)} %collective-permute-done.1), channel_id=1, replica_groups=mesh['gx'=4,'gy'=8] {'gy'}, dimensions={3}, use_global_device_ids=true | all-gather | bytes 589824 | tf_op jit(solution)/shard_map/all_gather | solution.py:131
  58.1 15.1 %all_gather.6 = f32[8,8,2,1024]{3,1,2,0:T(8,128)S(1)} all-gather(f32[8,8,2,128]{3,1,2,0:T(8,128)S(1)} %collective-permute-done), channel_id=1, replica_groups=mesh['gx'=4,'gy'=8] {'gy'}, dimensions={3}, use_global_device_ids=true | all-gather | bytes 589824 | tf_op jit(solution)/shard_map/all_gather | solution.py:130
  75.2 0.9 multiply_bitcast_fusion.2
  77.1 1.0 constant_dynamic-update-slice_fusion.8
  78.1 1.0 copy-done.16
  79.1 1.4 %fusion.21 = (f32[8,8,36,2]{3,1,2,0:T(8,128)}, f32[8,8,36,2]{3,1,2,0:T(8,128)S(1)}) fusion(f32[8,8,36,128]{3,1,2,0:T(8,128)S(1)} %get-tuple-element.87), kind=kLoop, calls=%fused_computation.205 | loop fusion | bytes 73728 | tf_op jit(solution)/shard_map/slice | solution.py:17
  80.5 1.8 %copy.194 = f32[8,8,36,2]{2,1,3,0:T(8,128)S(1)} copy(f32[8,8,36,2]{3,1,2,0:T(8,128)} %get-tuple-element.52) | data formatting | bytes 36864 | tf_op jit(solution)/shard_map/slice | solution.py:17
  82.7 1.2 %copy.196 = f32[8,8,36,2]{2,1,3,0:T(8,128)} copy(f32[8,8,36,2]{3,1,2,0:T(8,128)S(1)} %get-tuple-element.53) | data formatting | bytes 36864 | tf_op jit(solution)/shard_map/slice | solution.py:18
  83.9 3.4 %collective-permute-start.3 = (f32[8,8,36,2]{2,1,3,0:T(8,128)}, f32[8,8,36,2]{2,1,3,0:T(8,128)}, u32[]{:S(2)}, u32[]{:S(2)}) collective-permute-start(f32[8,8,36,2]{2,1,3,0:T(8,128)} %copy.196), channel_id=1, source_target_pairs={{1,0},{2,1},{3,2},{4,3},{5,4},{6,5},{7,6},{0,7},{9,8},{10,9},{11,1... | collective-permute-start | bytes 55304 | tf_op jit(solution)/shard_map/ppermute | solution.py:20
  90.4 1.1 copy-done.15
  91.8 1.2 %multiply_subtract_fusion.2 = f32[8,8,33,128]{3,1,2,0:T(8,128)} fusion(f32[8,8,33,128]{3,1,2,0:T(8,128)S(1)} %get-tuple-element.93, f32[8,8,33,128]{3,1,2,0:T(8,128)S(1)} %get-tuple-element.92, f32[8,8,33,128]{3,1,2,0:T(8,128)S(1)} %get-tuple-element.60, f32[8,8,33,128]{3,1,2,0:T(8,128)S(1)} %copy-done.19, f32[8,33,128]{2,0,1:T(8,128)S(1)} %get-tuple-element.5), kind=kLoop, calls=%fused_computation.29 | loop fusion | flops 1351680 | bytes 5541888 | tf_op jit(solution)/shard_map/sub | solution.py:74
  92.9 1.5 %copy.195 = f32[8,8,36,2]{3,1,2,0:T(8,128)S(1)} copy(f32[8,8,36,2]{2,1,3,0:T(8,128)} %collective-permute-done.2) | data formatting | bytes 36864 | tf_op jit(solution)/shard_map/ppermute | solution.py:19
  94.5 1.4 %copy.198 = f32[8,8,36,2]{3,1,2,0:T(8,128)S(1)} copy(f32[8,8,36,2]{2,1,3,0:T(8,128)} %collective-permute-done.3) | data formatting | bytes 36864 | tf_op jit(solution)/shard_map/ppermute | solution.py:20
  95.9 1.0 pad_maximum_fusion
  97.5 1.4 %minimum_multiply_fusion.1 = f32[8,8,32,130]{3,1,2,0:T(8,128)S(1)} fusion(f32[8,8,32,131]{3,1,2,0:T(8,128)S(1)} %slice_subtract_fusion), kind=kLoop, calls=%fused_computation.16 | loop fusion | flops 2129920 | bytes 3194880 | tf_op jit(solution)/shard_map/mul | solution.py:63
  99.0 1.5 %fusion.3 = (f32[8,8,32,129]{3,1,2,0:T(8,128)S(1)}, f32[8,8,32,129]{3,1,2,0:T(8,128)S(1)}) fusion(f32[8,8,32,130]{3,1,2,0:T(8,128)S(1)} %minimum_multiply_fusion.1, f32[8,8,36,128]{3,1,2,0:T(8,128)S(1)} %copy-done.3, f32[8,8,36,2]{3,1,2,0:T(8,128)S(1)} %copy.195, f32[8,8,36,2]{3,1,2,0:T(8,128)S(1)} %copy.198), kind=kLoop, calls=%fused_computation.9 | loop fusion | flops 1585152 | bytes 5443584 | tf_op jit(solution)/shard_map/add | solution.py:86
  105.1 4.8 %fusion.12 = f32[8,8,32,128]{3,1,2,0:T(8,128)S(1)} fusion(f32[8,9,32,128]{3,1,2,0:T(8,128)S(1)} %copy-done.7, f32[8,8,32,129]{3,1,2,0:T(8,128)S(1)} %multiply_subtract_fusion.1, f32[8,8,33,128]{3,1,2,0:T(8,128)S(1)} %copy-done.6, f32[8,8,32,128]{3,2,1,0:T(8,128)S(1)} %copy-done.20, f32[8,8,32,128]{3,2,1,0:T(8,128)} %slice_dynamic-update-slice_fusion.6, ...), kind=kLoop, calls=%fused_computation.37 | loop fusion | flops 2883584 | bytes 10485760 | tf_op jit(solution)/shard_map/add | solution.py:116
  109.9 1.2 %copy.207 = f32[8,8,32,128]{3,2,1,0:T(8,128)} copy(f32[8,8,32,128]{3,1,2,0:T(8,128)S(1)} %fusion.12) | data formatting | bytes 2097152 | tf_op jit(solution)/shard_map/add | solution.py:116
  (132 shorter events, 26.4 us)
Async XLA Ops:
  0.0 8.2 %copy-start.1 = (f32[8,8,32,128]{3,2,1,0:T(8,128)S(1)}, f32[8,8,32,128]{3,2,1,0:T(8,128)}, u32[]{:S(2)}) copy-start(f32[8,8,32,128]{3,2,1,0:T(8,128)} %param.5) | copy-start | bytes 3145732
  1.9 1.0 copy-start.4
  3.6 39.4 %collective-permute-start.1 = (f32[8,8,2,128]{3,1,2,0:T(8,128)}, f32[8,8,2,128]{3,1,2,0:T(8,128)S(1)}, u32[]{:S(2)}, u32[]{:S(2)}) collective-permute-start(f32[8,8,2,128]{3,1,2,0:T(8,128)} %get-tuple-element.78), channel_id=1, source_target_pairs={{8,0},{16,8},{24,16},{0,24},{9,1},{17,9},{25,17},{1,25},{10,2},{18... | collective-permute-start | bytes 196616 | tf_op jit(solution)/shard_map/ppermute | solution.py:20
  7.5 50.6 %collective-permute-start = (f32[8,8,2,128]{3,1,2,0:T(8,128)}, f32[8,8,2,128]{3,1,2,0:T(8,128)S(1)}, u32[]{:S(2)}, u32[]{:S(2)}) collective-permute-start(f32[8,8,2,128]{3,1,2,0:T(8,128)} %get-tuple-element.79), channel_id=1, source_target_pairs={{0,8},{8,16},{16,24},{24,0},{1,9},{9,17},{17,25},{25,1},{2,10},{10... | collective-permute-start | bytes 196616 | tf_op jit(solution)/shard_map/ppermute | solution.py:19
  14.5 1.5 %copy-start.8 = (f32[8,9,32,128]{3,2,1,0:T(8,128)S(1)}, f32[8,9,32,128]{3,2,1,0:T(8,128)}, u32[]{:S(2)}) copy-start(f32[8,9,32,128]{3,2,1,0:T(8,128)} %get-tuple-element.80) | copy-start | bytes 3538948
  14.5 1.6 %copy-start.9 = (f32[8,9,32,128]{3,2,1,0:T(8,128)S(1)}, f32[8,9,32,128]{3,2,1,0:T(8,128)}, u32[]{:S(2)}) copy-start(f32[8,9,32,128]{3,2,1,0:T(8,128)} %get-tuple-element.81) | copy-start | bytes 3538948
  18.3 8.5 %copy-start = (f32[8,9,32,128]{3,1,2,0:T(8,128)}, f32[8,9,32,128]{3,1,2,0:T(8,128)S(1)}, u32[]{:S(2)}) copy-start(f32[8,9,32,128]{3,1,2,0:T(8,128)S(1)} %get-tuple-element.48) | copy-start | bytes 3538948
  21.3 3.2 %copy-start.10 = (f32[8,9,32,128]{3,1,2,0:T(8,128)}, f32[8,9,32,128]{3,1,2,0:T(8,128)S(1)}, u32[]{:S(2)}) copy-start(f32[8,9,32,128]{3,1,2,0:T(8,128)S(1)} %get-tuple-element.43) | copy-start | bytes 3538948
  25.4 5.2 %copy-start.12 = (f32[8,9,32,128]{3,1,2,0:T(8,128)}, f32[8,9,32,128]{3,1,2,0:T(8,128)S(1)}, u32[]{:S(2)}) copy-start(f32[8,9,32,128]{3,1,2,0:T(8,128)S(1)} %get-tuple-element.45) | copy-start | bytes 3538948
  32.9 5.4 %copy-start.11 = (f32[8,9,32,128]{3,1,2,0:T(8,128)S(1)}, f32[8,9,32,128]{3,1,2,0:T(8,128)}, u32[]{:S(2)}) copy-start(f32[8,9,32,128]{3,1,2,0:T(8,128)} %copy-done.10) | copy-start | bytes 3538948
  32.9 5.4 %copy-start.13 = (f32[8,9,32,128]{3,1,2,0:T(8,128)S(1)}, f32[8,9,32,128]{3,1,2,0:T(8,128)}, u32[]{:S(2)}) copy-start(f32[8,9,32,128]{3,1,2,0:T(8,128)} %copy-done.12) | copy-start | bytes 3538948
  73.2 1.2 %copy-start.5 = (f32[8,8,32,128]{3,1,2,0:T(8,128)S(1)}, f32[8,8,32,128]{3,1,2,0:T(8,128)}, u32[]{:S(2)}) copy-start(f32[8,8,32,128]{3,1,2,0:T(8,128)} %copy-done.4) | copy-start | bytes 3145732
  74.3 4.8 %copy-start.2 = (f32[8,8,36,128]{3,1,2,0:T(8,128)}, f32[8,8,36,128]{3,1,2,0:T(8,128)S(1)}, u32[]{:S(2)}) copy-start(f32[8,8,36,128]{3,1,2,0:T(8,128)S(1)} %get-tuple-element.87) | copy-start | bytes 3538948
  76.9 1.2 %copy-start.18 = (f32[8,8,33,128]{3,1,2,0:T(8,128)}, f32[8,8,33,128]{3,1,2,0:T(8,128)S(1)}, u32[]{:S(2)}) copy-start(f32[8,8,33,128]{3,1,2,0:T(8,128)S(1)} %get-tuple-element.8) | copy-start | bytes 3244036
  78.1 1.0 copy-start.16
  82.3 10.7 %collective-permute-start.2 = (f32[8,8,36,2]{2,1,3,0:T(8,128)S(1)}, f32[8,8,36,2]{2,1,3,0:T(8,128)}, u32[]{:S(2)}, u32[]{:S(2)}) collective-permute-start(f32[8,8,36,2]{2,1,3,0:T(8,128)S(1)} %copy.194), channel_id=1, source_target_pairs={{0,1},{1,2},{2,3},{3,4},{4,5},{5,6},{6,7},{7,0},{8,9},{9,10},{10,1... | collective-permute-start | bytes 55304 | tf_op jit(solution)/shard_map/ppermute | solution.py:19
  83.9 5.6 %copy-start.22 = (f32[1,8,33,128]{3,1,2,0:T(8,128)S(1)}, f32[1,8,33,128]{3,1,2,0:T(8,128)}, u32[]{:S(2)}) copy-start(f32[1,8,33,128]{3,1,2,0:T(8,128)} %get-tuple-element.9) | copy-start | bytes 405508
  83.9 6.3 %copy-start.14 = (f32[8,8,33,128]{3,1,2,0:T(8,128)S(1)}, f32[8,8,33,128]{3,1,2,0:T(8,128)}, u32[]{:S(2)}) copy-start(f32[8,8,33,128]{3,1,2,0:T(8,128)} %get-tuple-element.66) | copy-start | bytes 3244036
  83.9 6.3 %copy-start.17 = (f32[8,8,33,128]{3,1,2,0:T(8,128)S(1)}, f32[8,8,33,128]{3,1,2,0:T(8,128)}, u32[]{:S(2)}) copy-start(f32[8,8,33,128]{3,1,2,0:T(8,128)} %copy-done.16) | copy-start | bytes 3244036
  83.9 10.6 %collective-permute-start.3 = (f32[8,8,36,2]{2,1,3,0:T(8,128)}, f32[8,8,36,2]{2,1,3,0:T(8,128)}, u32[]{:S(2)}, u32[]{:S(2)}) collective-permute-start(f32[8,8,36,2]{2,1,3,0:T(8,128)} %copy.196), channel_id=1, source_target_pairs={{1,0},{2,1},{3,2},{4,3},{5,4},{6,5},{7,6},{0,7},{9,8},{10,9},{11,1... | collective-permute-start | bytes 55304 | tf_op jit(solution)/shard_map/ppermute | solution.py:20
  88.8 1.6 %copy-start.21 = (f32[1,8,33,128]{3,1,2,0:T(8,128)S(1)}, f32[1,8,33,128]{3,1,2,0:T(8,128)}, u32[]{:S(2)}) copy-start(f32[1,8,33,128]{3,1,2,0:T(8,128)} %get-tuple-element.11) | copy-start | bytes 405508
  90.2 1.2 %copy-start.15 = (f32[8,8,33,128]{3,1,2,0:T(8,128)S(1)}, f32[8,8,33,128]{3,1,2,0:T(8,128)}, u32[]{:S(2)}) copy-start(f32[8,8,33,128]{3,1,2,0:T(8,128)} %constant_dynamic-update-slice_fusion.21) | copy-start | bytes 3244036
  90.2 1.6 %copy-start.19 = (f32[8,8,33,128]{3,1,2,0:T(8,128)S(1)}, f32[8,8,33,128]{3,1,2,0:T(8,128)}, u32[]{:S(2)}) copy-start(f32[8,8,33,128]{3,1,2,0:T(8,128)} %get-tuple-element.54) | copy-start | bytes 3244036
  92.9 2.9 %copy-start.3 = (f32[8,8,36,128]{3,1,2,0:T(8,128)S(1)}, f32[8,8,36,128]{3,1,2,0:T(8,128)}, u32[]{:S(2)}) copy-start(f32[8,8,36,128]{3,1,2,0:T(8,128)} %copy-done.2) | copy-start | bytes 3538948
  102.9 1.2 %copy-start.6 = (f32[8,8,33,128]{3,1,2,0:T(8,128)S(1)}, f32[8,8,33,128]{3,1,2,0:T(8,128)}, u32[]{:S(2)}) copy-start(f32[8,8,33,128]{3,1,2,0:T(8,128)} %multiply_subtract_fusion.2) | copy-start | bytes 3244036
  102.9 1.9 %copy-start.7 = (f32[8,9,32,128]{3,1,2,0:T(8,128)S(1)}, f32[8,9,32,128]{3,1,2,0:T(8,128)}, u32[]{:S(2)}) copy-start(f32[8,9,32,128]{3,1,2,0:T(8,128)} %multiply_subtract_fusion) | copy-start | bytes 3538948
  102.9 2.2 %copy-start.20 = (f32[8,8,32,128]{3,2,1,0:T(8,128)S(1)}, f32[8,8,32,128]{3,2,1,0:T(8,128)}, u32[]{:S(2)}) copy-start(f32[8,8,32,128]{3,2,1,0:T(8,128)} %param.4) | copy-start | bytes 3145732
where the time goes:
time: 112 us; the launch traced here: 111 us
  other arithmetic  43.6 us (39%)
  blocking collectives  30.1 us (27%)
  local copies, waits for them, and re-layouts  27.7 us (25%)
  starting transfers between devices  7.7 us (7%)
  between operations  1.96 us (2%)
    all_gather x1, blocking collectives, on_device(): lax.all_gather(inner_src, 'gy', axis=3, tiled=True)  15.1 us
    all_gather x1, blocking collectives, on_device(): lax.all_gather(outer_src, 'gy', axis=3, tiled=True)  15 us
    unnamed x50, other arithmetic  14.1 us
    unnamed x58, local copies, waits for them, and re-layouts  14 us
    ppermute x2, starting transfers between devices, with_halo(): after = lax.ppermute(first, axis, down)  7.32 us
    sub x3, other arithmetic, rusanov(): 0.5 * (flux_left + flux_right) - 0.5 * speed * (cons_right - cons_left)  5.88 us
    add x1, other arithmetic, section_update(): return 0.5 * old + 0.5 * (conserved(core) + time_step * rates)  4.85 us
    add x3, other arithmetic, sweep(): left = take(padded, 1, length - 2) + 0.5 * take(slope, 0, length - 3)  3.84 us
  transfers between devices with their start and end apart: 4, of which 0 were waited for; matrix products, arithmetic and copies ran while one was open for 37% of the time, Pallas kernels for 0%

commit v1 on v0

--- a/solution.py
+++ b/solution.py
@@ -7,6 +7,18 @@
 omega_rate = 1.0
 shear_rate = 1.5
 time_step = 0.1
+
+
+def doubled_up(value, axis, dim):
+    ways, here = (lax.axis_size(axis), lax.axis_index(axis))
+    grown, reach = (value, 1)
+    while reach < ways:
+        theirs = lax.ppermute(grown, axis, [(d, d ^ reach) for d in range(ways)])
+        mine_first = jnp.concatenate([grown, theirs], axis=dim)
+        theirs_first = jnp.concatenate([theirs, grown], axis=dim)
+        grown = jnp.where(here & reach == 0, mine_first, theirs_first)
+        reach = 2 * reach
+    return grown
 
 
 def with_halo(shard, sides, width):
@@ -127,7 +139,7 @@
     inner_src = padded[:, :, 0:2, 2:-2]
     outer_src = padded[:, :, -2:, 2:-2]
     inner_cycle, outer_cycle = (
-        lax.all_gather(inner_src, "gy", axis=3, tiled=True),
+        doubled_up(inner_src, "gy", 3),
         lax.all_gather(outer_src, "gy", axis=3, tiled=True),
     )
     position = lax.axis_index("gy") * cells

time: 112 us -> 97.7 us (0.87)
  blocking collectives: 30.1 us -> 22.1 us
  local copies, waits for them, and re-layouts: 27.7 us -> 19.9 us
  other arithmetic: 43.6 us -> 38.4 us
  starting transfers between devices: 7.7 us -> 12.5 us
  waiting for transfers between devices: 0.01 us -> 2.2 us
    all_gather x1 -> x0, blocking collectives: 15.1 us -> none  [on_device(): lax.all_gather(inner_src, 'gy', axis=3, tiled=True)]
    all_gather x1, blocking collectives: 15 us -> 22.1 us  [on_device(): lax.all_gather(outer_src, 'gy', axis=3, tiled=True)]
    unnamed x58 -> x42, local copies, waits for them, and re-layouts: 14 us -> 7.3 us
    ppermute x0 -> x3, starting transfers between devices: none -> 4.94 us  [doubled_up(): theirs = lax.ppermute(grown, axis, [(d, d ^ reach) for d in range(ways)])]
    ppermute x2, starting transfers between devices: 7.32 us -> 4.22 us  [with_halo(): after = lax.ppermute(first, axis, down)]
    another operation x4, local copies, waits for them, and re-layouts: 3.5 us -> 0.43 us  [conserved(): jnp.stack([rho, rho * prims[1], rho * prims[2], rho * prims[3], energy, p...]
    ppermute x2, starting transfers between devices: 0.39 us -> 3.37 us  [with_halo(): before = lax.ppermute(last, axis, up)]
    unnamed x50, other arithmetic: 14.1 us -> 11.5 us
  transfers between devices with their start and end apart: 4 -> 7, of which waited for: 0 -> 2; matrix products, arithmetic and copies ran while one was open for 37% -> 25% of each run, Pallas kernels for 0% -> 0%
where the time goes in v1:
time: 97.7 us; the launch traced here: 97.2 us
  other arithmetic  38.4 us (39%)
  blocking collectives  22.1 us (23%)
  local copies, waits for them, and re-layouts  19.9 us (20%)
  starting transfers between devices  12.5 us (13%)
  waiting for transfers between devices  2.2 us (2%)
  between operations  2.13 us (2%)
    all_gather x1, blocking collectives, on_device(): lax.all_gather(outer_src, 'gy', axis=3, tiled=True)  22.1 us
    unnamed x50, other arithmetic  11.5 us
    unnamed x42, local copies, waits for them, and re-layouts  7.3 us
    sub x3, other arithmetic, rusanov(): 0.5 * (flux_left + flux_right) - 0.5 * speed * (cons_right - cons_left)  5.4 us
    ppermute x3, starting transfers between devices, doubled_up(): theirs = lax.ppermute(grown, axis, [(d, d ^ reach) for d in range(ways)])  4.94 us
    ppermute x2, starting transfers between devices, with_halo(): after = lax.ppermute(first, axis, down)  4.22 us
    add x3, other arithmetic, sweep(): left = take(padded, 1, length - 2) + 0.5 * take(slope, 0, length - 3)  3.81 us
    slice x2, local copies, waits for them, and re-layouts, with_halo(): last = lax.slice_in_dim(shard, length - width, length, axis=dim)  3.62 us
  transfers between devices with their start and end apart: 7, of which 2 were waited for; matrix products, arithmetic and copies ran while one was open for 25% of the time, Pallas kernels for 0%

profile of v1, /device:TPU:0, one launch (start us, length us, event | category | flops | bytes accessed | tf_op | source)
XLA Modules:
  0.0 97.2 jit_solution(2512815240417189124)
XLA Ops:
  0.0 1.9 %copy.190 = f32[8,8,32,128]{3,1,2,0:T(8,128)S(1)} copy(f32[8,8,32,128]{3,2,1,0:T(8,128)} %param.5) | data formatting | bytes 2097152 | tf_op args[1]
  2.0 3.0 %collective-permute-start = (f32[8,8,2,128]{3,1,2,0:T(8,128)S(1)}, f32[8,8,2,128]{3,1,2,0:T(8,128)S(1)}, u32[]{:S(2)}, u32[]{:S(2)}) collective-permute-start(f32[8,8,2,128]{3,1,2,0:T(8,128)S(1)} %get-tuple-element.79), channel_id=1, source_target_pairs={{0,8},{8,16},{16,24},{24,0},{1,9},{9,17},{17,25},{25,1},{2,10},{10... | collective-permute-start | bytes 196616 | tf_op jit(solution)/shard_map/ppermute | solution.py:31
  4.9 1.0 %collective-permute-start.4 = (f32[8,8,2,128]{3,1,2,0:T(8,128)S(1)}, f32[8,8,2,128]{3,1,2,0:T(8,128)S(1)}, u32[]{:S(2)}, u32[]{:S(2)}) collective-permute-start(f32[8,8,2,128]{3,1,2,0:T(8,128)S(1)} %get-tuple-element.78), channel_id=1, source_target_pairs={{8,0},{16,8},{24,16},{0,24},{9,1},{17,9},{25,17},{1,25},{10,2},{18... | collective-permute-start | bytes 196616 | tf_op jit(solution)/shard_map/ppermute | solution.py:32
  6.9 2.1 %copy_subtract_fusion = f32[8,11,32,128]{3,1,2,0:T(8,128)S(1)} fusion(f32[8,11,32,128]{3,2,1,0:T(8,128)S(1)} %get-tuple-element.51, f32[8,11,32,128]{3,2,1,0:T(8,128)S(1)} %get-tuple-element.50), kind=kLoop, calls=%fused_computation.12 | loop fusion | flops 360448 | bytes 4325376 | tf_op jit(solution)/shard_map/sub | solution.py:96
  8.9 1.5 %minimum_multiply_fusion = f32[8,10,32,128]{3,1,2,0:T(8,128)S(1)} fusion(f32[8,11,32,128]{3,1,2,0:T(8,128)S(1)} %copy_subtract_fusion), kind=kLoop, calls=%fused_computation.14 | loop fusion | flops 2621440 | bytes 3932160 | tf_op jit(solution)/shard_map/mul | solution.py:75
  10.4 2.2 %fusion.1 = (f32[8,9,32,128]{3,1,2,0:T(8,128)S(1)}, f32[8,9,32,128]{3,1,2,0:T(8,128)S(1)}) fusion(f32[8,10,32,128]{3,1,2,0:T(8,128)S(1)} %minimum_multiply_fusion, f32[8,9,32,128]{3,2,1,0:T(8,128)S(1)} %get-tuple-element.80, f32[8,9,32,128]{3,2,1,0:T(8,128)S(1)} %get-tuple-element.81), kind=kLoop, calls=%fused_computation.4 | loop fusion | flops 1179648 | bytes 7077888 | tf_op jit(solution)/shard_map/add | solution.py:98
  15.3 1.9 %multiply_subtract_fusion = f32[8,9,32,128]{3,1,2,0:T(8,128)} fusion(f32[8,9,32,128]{3,1,2,0:T(8,128)S(1)} %get-tuple-element.89, f32[8,9,32,128]{3,1,2,0:T(8,128)S(1)} %get-tuple-element.88, f32[8,9,32,128]{3,1,2,0:T(8,128)S(1)} %get-tuple-element.45, f32[8,9,32,128]{3,1,2,0:T(8,128)S(1)} %get-tuple-element.43, f32[9,32,128]{2,0,1:T(8,128)S(1)} %get-tuple-element.19), kind=kLoop, calls=%fused_computation.13 | loop fusion | flops 1474560 | bytes 6045696 | tf_op jit(solution)/shard_map/sub | solution.py:86
  17.5 1.0 copy-done.10
  18.6 2.1 %collective-permute-start.2 = (f32[8,8,2,256]{3,1,2,0:T(8,128)S(1)}, f32[8,8,2,256]{3,1,2,0:T(8,128)}, u32[]{:S(2)}, u32[]{:S(2)}) collective-permute-start(f32[8,8,2,256]{3,1,2,0:T(8,128)S(1)} %maximum_select_fusion.2), channel_id=1, source_target_pairs={{0,2},{1,3},{2,0},{3,1},{4,6},{5,7},{6,4},{7,5},{8,10},{9,11},{10,... | collective-permute-start | bytes 393224 | tf_op jit(solution)/shard_map/ppermute | solution.py:16
  22.7 2.0 %collective-permute-done.2 = f32[8,8,2,256]{3,1,2,0:T(8,128)} collective-permute-done((f32[8,8,2,256]{3,1,2,0:T(8,128)S(1)}, f32[8,8,2,256]{3,1,2,0:T(8,128)}, u32[]{:S(2)}, u32[]{:S(2)}) %collective-permute-start.2) | collective-permute-done | bytes 131104 | tf_op jit(solution)/shard_map/ppermute | solution.py:16
  24.8 1.0 %maximum_select_fusion.1 = f32[8,8,2,512]{3,1,2,0:T(8,128)S(1)} fusion(f32[8,8,2,256]{3,1,2,0:T(8,128)} %collective-permute-done.2, f32[8,8,2,256]{3,1,2,0:T(8,128)S(1)} %maximum_select_fusion.2, pred[]{:T(512)S(6)} %eq.21), kind=kLoop, calls=%fused_computation.53 | loop fusion | flops 196608 | bytes 524289 | tf_op jit(solution)/shard_map/jit(_where)/select_n | solution.py:19
  25.8 2.8 %collective-permute-start.3 = (f32[8,8,2,512]{3,1,2,0:T(8,128)S(1)}, f32[8,8,2,512]{3,1,2,0:T(8,128)S(1)}, u32[]{:S(2)}, u32[]{:S(2)}) collective-permute-start(f32[8,8,2,512]{3,1,2,0:T(8,128)S(1)} %maximum_select_fusion.1), channel_id=1, source_target_pairs={{0,4},{1,5},{2,6},{3,7},{4,0},{5,1},{6,2},{7,3},{8,12},{9,13},{10,... | collective-permute-start | bytes 786440 | tf_op jit(solution)/shard_map/ppermute | solution.py:16
  28.6 22.1 %all_gather.3 = f32[8,8,2,1024]{3,1,2,0:T(8,128)S(1)} all-gather(f32[8,8,2,128]{3,1,2,0:T(8,128)S(1)} %collective-permute-done.4), channel_id=1, replica_groups=mesh['gx'=4,'gy'=8] {'gy'}, dimensions={3}, use_global_device_ids=true | all-gather | bytes 589824 | tf_op jit(solution)/shard_map/all_gather | solution.py:143
  52.6 0.8 copy-done.3
  53.5 1.0 %multiply_bitcast_fusion.2 = (f32[8,33,128]{2,0,1:T(8,128)S(1)}, f32[1,8,33,128]{3,1,2,0:T(8,128)S(1)}, f32[1,8,33,128]{3,1,2,0:T(8,128)S(1)}, f32[8,8,33,128]{3...) fusion(f32[8,8,33,128]{3,1,2,0:T(8,128)S(1)} %get-tuple-element.29, ...), kind=kLoop, calls=%fused_computation.180 | loop fusion | flops 1486845 | bytes 2433024 | tf_op jit(solution)/shard_map/mul | solution.py:86
  56.6 0.8 constant_dynamic-update-slice_fusion.16
  59.5 0.8 constant_dynamic-update-slice_fusion.8
  60.4 1.8 %fusion.21 = (f32[8,8,36,2]{3,1,2,0:T(8,128)}, f32[8,8,36,2]{3,1,2,0:T(8,128)}) fusion(f32[8,8,36,128]{3,1,2,0:T(8,128)S(1)} %get-tuple-element.87), kind=kLoop, calls=%fused_computation.208 | loop fusion | bytes 73728 | tf_op jit(solution)/shard_map/slice | solution.py:29
  62.2 1.8 %copy.196 = f32[8,8,36,2]{2,1,3,0:T(8,128)S(1)} copy(f32[8,8,36,2]{3,1,2,0:T(8,128)} %get-tuple-element.52) | data formatting | bytes 36864 | tf_op jit(solution)/shard_map/slice | solution.py:29
  64.4 2.4 %copy.198 = f32[8,8,36,2]{2,1,3,0:T(8,128)} copy(f32[8,8,36,2]{3,1,2,0:T(8,128)} %get-tuple-element.53) | data formatting | bytes 36864 | tf_op jit(solution)/shard_map/slice | solution.py:30
  66.8 3.2 %collective-permute-start.6 = (f32[8,8,36,2]{2,1,3,0:T(8,128)}, f32[8,8,36,2]{2,1,3,0:T(8,128)}, u32[]{:S(2)}, u32[]{:S(2)}) collective-permute-start(f32[8,8,36,2]{2,1,3,0:T(8,128)} %copy.198), channel_id=1, source_target_pairs={{1,0},{2,1},{3,2},{4,3},{5,4},{6,5},{7,6},{0,7},{9,8},{10,9},{11,1... | collective-permute-start | bytes 55304 | tf_op jit(solution)/shard_map/ppermute | solution.py:32
  70.0 0.7 constant_dynamic-update-slice_fusion.15
  70.7 0.7 constant_dynamic-update-slice_fusion.14
  71.5 0.7 constant_dynamic-update-slice_fusion.13
  75.1 2.9 %multiply_subtract_fusion.2 = f32[8,8,33,128]{3,1,2,0:T(8,128)} fusion(f32[8,8,33,128]{3,1,2,0:T(8,128)S(1)} %get-tuple-element.93, f32[8,8,33,128]{3,1,2,0:T(8,128)S(1)} %get-tuple-element.92, f32[8,8,33,128]{3,1,2,0:T(8,128)} %get-tuple-element.60, f32[8,8,33,128]{3,1,2,0:T(8,128)} %get-tuple-element.54, f32[8,33,128]{2,0,1:T(8,128)S(1)} %get-tuple-element.5), kind=kLoop, calls=%fused_computation.29 | loop fusion | flops 1351680 | bytes 5541888 | tf_op jit(solution)/shard_map/sub | solution.py:86
  78.0 1.4 %copy.197 = f32[8,8,36,2]{3,1,2,0:T(8,128)S(1)} copy(f32[8,8,36,2]{2,1,3,0:T(8,128)} %collective-permute-done.5) | data formatting | bytes 36864 | tf_op jit(solution)/shard_map/ppermute | solution.py:31
  79.4 2.4 %copy.200 = f32[8,8,36,2]{3,1,2,0:T(8,128)} copy(f32[8,8,36,2]{2,1,3,0:T(8,128)} %collective-permute-done.6) | data formatting | bytes 36864 | tf_op jit(solution)/shard_map/ppermute | solution.py:32
  81.8 2.2 %pad_maximum_fusion = f32[8,8,36,132]{3,1,2,0:T(8,128)S(1)} fusion(f32[8,8,36,2]{3,1,2,0:T(8,128)} %copy.200, f32[8,8,36,128]{3,1,2,0:T(8,128)S(1)} %get-tuple-element.87, f32[8,8,36,2]{3,1,2,0:T(8,128)S(1)} %copy.197), kind=kLoop, calls=%fused_computation | loop fusion | flops 608256 | bytes 2433024 | tf_op jit(solution)/shard_map/concatenate | solution.py:33
  84.7 1.4 %minimum_multiply_fusion.1 = f32[8,8,32,130]{3,1,2,0:T(8,128)S(1)} fusion(f32[8,8,32,131]{3,1,2,0:T(8,128)S(1)} %slice_subtract_fusion), kind=kLoop, calls=%fused_computation.16 | loop fusion | flops 2129920 | bytes 3194880 | tf_op jit(solution)/shard_map/mul | solution.py:75
  86.2 1.5 %fusion.3 = (f32[8,8,32,129]{3,1,2,0:T(8,128)S(1)}, f32[8,8,32,129]{3,1,2,0:T(8,128)S(1)}) fusion(f32[8,8,32,130]{3,1,2,0:T(8,128)S(1)} %minimum_multiply_fusion.1, f32[8,8,36,128]{3,1,2,0:T(8,128)S(1)} %get-tuple-element.87, f32[8,8,36,2]{3,1,2,0:T(8,128)S(1)} %copy.197, f32[8,8,36,2]{3,1,2,0:T(8,128)S(1)} %copy-done.1), kind=kLoop, calls=%fused_computation.9 | loop fusion | flops 1585152 | bytes 5443584 | tf_op jit(solution)/shard_map/add | solution.py:98
  92.9 3.2 %fusion.12 = f32[8,8,32,128]{3,1,2,0:T(8,128)S(1)} fusion(f32[8,9,32,128]{3,1,2,0:T(8,128)S(1)} %copy-done.5, f32[8,8,32,129]{3,1,2,0:T(8,128)S(1)} %multiply_subtract_fusion.1, f32[8,8,33,128]{3,1,2,0:T(8,128)S(1)} %copy-done.4, f32[8,8,32,128]{3,2,1,0:T(8,128)S(1)} %copy-done.12, f32[8,8,32,128]{3,2,1,0:T(8,128)S(1)} %copy-done.9, ...), kind=kLoop, calls=%fused_computation.37 | loop fusion | flops 2883584 | bytes 10485760 | tf_op jit(solution)/shard_map/add | solution.py:128
  96.1 1.2 %copy.209 = f32[8,8,32,128]{3,2,1,0:T(8,128)} copy(f32[8,8,32,128]{3,1,2,0:T(8,128)S(1)} %fusion.12) | data formatting | bytes 2097152 | tf_op jit(solution)/shard_map/add | solution.py:128
  (124 shorter events, 19.3 us)
Async XLA Ops:
  0.0 6.0 %copy-start = (f32[8,8,32,128]{3,2,1,0:T(8,128)S(1)}, f32[8,8,32,128]{3,2,1,0:T(8,128)}, u32[]{:S(2)}) copy-start(f32[8,8,32,128]{3,2,1,0:T(8,128)} %param.5) | copy-start | bytes 3145732
  1.9 50.0 %copy-start.2 = (f32[8,8,32,128]{3,1,2,0:T(8,128)}, f32[8,8,32,128]{3,1,2,0:T(8,128)S(1)}, u32[]{:S(2)}) copy-start(f32[8,8,32,128]{3,1,2,0:T(8,128)S(1)} %copy.190) | copy-start | bytes 3145732
  2.0 15.3 %collective-permute-start = (f32[8,8,2,128]{3,1,2,0:T(8,128)S(1)}, f32[8,8,2,128]{3,1,2,0:T(8,128)S(1)}, u32[]{:S(2)}, u32[]{:S(2)}) collective-permute-start(f32[8,8,2,128]{3,1,2,0:T(8,128)S(1)} %get-tuple-element.79), channel_id=1, source_target_pairs={{0,8},{8,16},{16,24},{24,0},{1,9},{9,17},{17,25},{25,1},{2,10},{10... | collective-permute-start | bytes 196616 | tf_op jit(solution)/shard_map/ppermute | solution.py:31
  4.9 23.7 %collective-permute-start.4 = (f32[8,8,2,128]{3,1,2,0:T(8,128)S(1)}, f32[8,8,2,128]{3,1,2,0:T(8,128)S(1)}, u32[]{:S(2)}, u32[]{:S(2)}) collective-permute-start(f32[8,8,2,128]{3,1,2,0:T(8,128)S(1)} %get-tuple-element.78), channel_id=1, source_target_pairs={{8,0},{16,8},{24,16},{0,24},{9,1},{17,9},{25,17},{1,25},{10,2},{18... | collective-permute-start | bytes 196616 | tf_op jit(solution)/shard_map/ppermute | solution.py:32
  17.3 1.3 %collective-permute-start.1 = (f32[8,8,2,128]{3,1,2,0:T(8,128)S(1)}, f32[8,8,2,128]{3,1,2,0:T(8,128)S(1)}, u32[]{:S(2)}, u32[]{:S(2)}) collective-permute-start(f32[8,8,2,128]{3,1,2,0:T(8,128)S(1)} %collective-permute-done), channel_id=1, source_target_pairs={{0,1},{1,0},{2,3},{3,2},{4,5},{5,4},{6,7},{7,6},{8,9},{9,8},{10,11... | collective-permute-start | bytes 196616 | tf_op jit(solution)/shard_map/ppermute | solution.py:16
  17.5 1.0 copy-start.10
  18.6 6.2 %collective-permute-start.2 = (f32[8,8,2,256]{3,1,2,0:T(8,128)S(1)}, f32[8,8,2,256]{3,1,2,0:T(8,128)}, u32[]{:S(2)}, u32[]{:S(2)}) collective-permute-start(f32[8,8,2,256]{3,1,2,0:T(8,128)S(1)} %maximum_select_fusion.2), channel_id=1, source_target_pairs={{0,2},{1,3},{2,0},{3,1},{4,6},{5,7},{6,4},{7,5},{8,10},{9,11},{10,... | collective-permute-start | bytes 393224 | tf_op jit(solution)/shard_map/ppermute | solution.py:16
  20.7 30.4 %copy-start.8 = (f32[8,8,32,128]{3,2,1,0:T(8,128)}, f32[8,8,32,128]{3,2,1,0:T(8,128)S(1)}, u32[]{:S(2)}) copy-start(f32[8,8,32,128]{3,2,1,0:T(8,128)S(1)} %slice_dynamic-update-slice_fusion.6) | copy-start | bytes 3145732
  25.8 25.1 %collective-permute-start.3 = (f32[8,8,2,512]{3,1,2,0:T(8,128)S(1)}, f32[8,8,2,512]{3,1,2,0:T(8,128)S(1)}, u32[]{:S(2)}, u32[]{:S(2)}) collective-permute-start(f32[8,8,2,512]{3,1,2,0:T(8,128)S(1)} %maximum_select_fusion.1), channel_id=1, source_target_pairs={{0,4},{1,5},{2,6},{3,7},{4,0},{5,1},{6,2},{7,3},{8,12},{9,13},{10,... | collective-permute-start | bytes 786440 | tf_op jit(solution)/shard_map/ppermute | solution.py:16
  52.1 1.2 %copy-start.3 = (f32[8,8,32,128]{3,1,2,0:T(8,128)S(1)}, f32[8,8,32,128]{3,1,2,0:T(8,128)}, u32[]{:S(2)}) copy-start(f32[8,8,32,128]{3,1,2,0:T(8,128)} %copy-done.2) | copy-start | bytes 3145732
  64.0 14.0 %collective-permute-start.5 = (f32[8,8,36,2]{2,1,3,0:T(8,128)S(1)}, f32[8,8,36,2]{2,1,3,0:T(8,128)}, u32[]{:S(2)}, u32[]{:S(2)}) collective-permute-start(f32[8,8,36,2]{2,1,3,0:T(8,128)S(1)} %copy.196), channel_id=1, source_target_pairs={{0,1},{1,2},{2,3},{3,4},{4,5},{5,6},{6,7},{7,0},{8,9},{9,10},{10,1... | collective-permute-start | bytes 55304 | tf_op jit(solution)/shard_map/ppermute | solution.py:31
  66.8 5.4 %copy-start.14 = (f32[1,8,33,128]{3,1,2,0:T(8,128)S(1)}, f32[1,8,33,128]{3,1,2,0:T(8,128)}, u32[]{:S(2)}) copy-start(f32[1,8,33,128]{3,1,2,0:T(8,128)} %get-tuple-element.9) | copy-start | bytes 405508
  66.8 6.1 %copy-start.6 = (f32[8,8,33,128]{3,1,2,0:T(8,128)S(1)}, f32[8,8,33,128]{3,1,2,0:T(8,128)}, u32[]{:S(2)}) copy-start(f32[8,8,33,128]{3,1,2,0:T(8,128)} %get-tuple-element.66) | copy-start | bytes 3244036
  66.8 12.6 %collective-permute-start.6 = (f32[8,8,36,2]{2,1,3,0:T(8,128)}, f32[8,8,36,2]{2,1,3,0:T(8,128)}, u32[]{:S(2)}, u32[]{:S(2)}) collective-permute-start(f32[8,8,36,2]{2,1,3,0:T(8,128)} %copy.198), channel_id=1, source_target_pairs={{1,0},{2,1},{3,2},{4,3},{5,4},{6,5},{7,6},{0,7},{9,8},{10,9},{11,1... | collective-permute-start | bytes 55304 | tf_op jit(solution)/shard_map/ppermute | solution.py:32
  71.5 3.5 %copy-start.13 = (f32[1,8,33,128]{3,1,2,0:T(8,128)S(1)}, f32[1,8,33,128]{3,1,2,0:T(8,128)}, u32[]{:S(2)}) copy-start(f32[1,8,33,128]{3,1,2,0:T(8,128)} %get-tuple-element.11) | copy-start | bytes 405508
  72.9 2.1 %copy-start.7 = (f32[8,8,33,128]{3,1,2,0:T(8,128)S(1)}, f32[8,8,33,128]{3,1,2,0:T(8,128)}, u32[]{:S(2)}) copy-start(f32[8,8,33,128]{3,1,2,0:T(8,128)} %constant_dynamic-update-slice_fusion.21) | copy-start | bytes 3244036
  84.7 1.5 %copy-start.1 = (f32[8,8,36,2]{3,1,2,0:T(8,128)S(1)}, f32[8,8,36,2]{3,1,2,0:T(8,128)}, u32[]{:S(2)}) copy-start(f32[8,8,36,2]{3,1,2,0:T(8,128)} %copy.200) | copy-start | bytes 55300
  90.0 1.2 %copy-start.4 = (f32[8,8,33,128]{3,1,2,0:T(8,128)S(1)}, f32[8,8,33,128]{3,1,2,0:T(8,128)}, u32[]{:S(2)}) copy-start(f32[8,8,33,128]{3,1,2,0:T(8,128)} %multiply_subtract_fusion.2) | copy-start | bytes 3244036
  90.1 1.9 %copy-start.5 = (f32[8,9,32,128]{3,1,2,0:T(8,128)S(1)}, f32[8,9,32,128]{3,1,2,0:T(8,128)}, u32[]{:S(2)}) copy-start(f32[8,9,32,128]{3,1,2,0:T(8,128)} %multiply_subtract_fusion) | copy-start | bytes 3538948
  90.1 2.2 %copy-start.9 = (f32[8,8,32,128]{3,2,1,0:T(8,128)S(1)}, f32[8,8,32,128]{3,2,1,0:T(8,128)}, u32[]{:S(2)}) copy-start(f32[8,8,32,128]{3,2,1,0:T(8,128)} %copy-done.8) | copy-start | bytes 3145732
  90.1 2.5 %copy-start.11 = (f32[8,8,32,128]{3,2,1,0:T(8,128)S(1)}, f32[8,8,32,128]{3,2,1,0:T(8,128)}, u32[]{:S(2)}) copy-start(f32[8,8,32,128]{3,2,1,0:T(8,128)} %constant_dynamic-update-slice_fusion.58) | copy-start | bytes 3145732
  90.1 2.8 %copy-start.12 = (f32[8,8,32,128]{3,2,1,0:T(8,128)S(1)}, f32[8,8,32,128]{3,2,1,0:T(8,128)}, u32[]{:S(2)}) copy-start(f32[8,8,32,128]{3,2,1,0:T(8,128)} %param.4) | copy-start | bytes 3145732
